TPU v7x, 256 devices: a whole 4x4x8 slice. The times are simulated.
256 devices in a mesh: kx: 8 (over z), ht: 8 (over y, core), real: 4 (over x).
Axes of the slice: x: 4, y: 4, z: 8, core: 2. Of those that a mesh axis runs over, the one named last changes fastest.
Arguments:
- velocity: float32 [3, 4, 32, 512, 128], P(None, 'real', 'kx', 'ht'), may hold values from -6 to 6
- low_index: int32 [8], replicated, may hold values from 0 to 31, as said below
- neighbours: int32 [32, 8], P('kx'), may hold values from 0 to 31, as said below
- owner_map: int32 [64], replicated, may hold values from 0 to 63, each once
- mode_counts: int32 [32], P('kx'), may hold values from 16 to 64
- helmholtz: float32 [64, 512, 512], P(('kx', 'ht')), may hold values from -0.25 to 0.25
Outputs:
- velocity_next: float32 [3, 4, 32, 512, 128], P(None, 'real', 'kx', 'ht')
Inputs may be any that keep to these rules, and one draw needn't show every extreme that they name: `low_index`: distinct values. neighbours[m, j] lies within 4 modes of m, counting circularly over the 32 modes; offsets of + 4 and - 4 both occur.
All inputs are finite; a program needn't handle non-finite values.
Results may differ from a plain program's by a relative error of at most 0.0001.
Values sent between devices are 32-bit elements; how exact they have to be, the bound alone decides.
A program may use at most 64 MiB of HBM per device.

v0:
```python
import jax
import jax.numpy as jnp
from jax import lax
from jax.sharding import PartitionSpec as P

dt_step = 0.1


def extended_2(block, sides, width):
    for axis, dim in sides:
        count = lax.axis_size(axis)
        forward = [(i, i + 1) for i in range(count - 1)]
        forward.append((count - 1, 0))
        backward = [(target, source) for source, target in forward]
        low = lax.ppermute(
            lax.slice_in_dim(block, block.shape[dim] - width, None, axis=dim), axis, forward
        )
        high = lax.ppermute(lax.slice_in_dim(block, 0, width, axis=dim), axis, backward)
        block = jnp.concatenate([low, block, high], axis=dim)
    return block


def spanwise_tables(mode_count, point_count):
    column_ids = jnp.arange(2 * mode_count)
    wavenumber = (column_ids // 2).astype(jnp.float32)
    imag_part = column_ids % 2
    positions = 2.0 * jnp.pi * jnp.arange(point_count).astype(jnp.float32) / point_count
    phases = wavenumber[:, None] * positions[None, :]
    forward = jnp.where(imag_part[:, None] == 0, jnp.cos(phases), -jnp.sin(phases)) / jnp.sqrt(
        jnp.float32(mode_count)
    )
    backward = forward.T * (2.0 * mode_count / point_count)
    return (forward, backward)


def apply_inverse(block, helmholtz, kx_count, ht_count, slots_dev, rows_ht):
    components, reals_dev, band_modes = (block.shape[0], block.shape[1], block.shape[2])
    regrouped = block.reshape(
        components, reals_dev, band_modes, kx_count, ht_count, slots_dev, 2, rows_ht
    )
    regrouped = regrouped.transpose(0, 1, 3, 2, 5, 6, 4, 7)
    regrouped = regrouped.reshape(
        components, reals_dev, kx_count * band_modes, slots_dev, 2, ht_count * rows_ht
    )
    solved = jnp.einsum("syx,crmspx->crmspy", helmholtz, regrouped, precision=lax.Precision.HIGHEST)
    solved = solved.reshape(
        components, reals_dev, kx_count, band_modes, slots_dev, 2, ht_count, rows_ht
    )
    solved = solved.transpose(0, 1, 3, 2, 6, 4, 5, 7)
    return solved.reshape(block.shape)


def local(velocity, low_index, neighbours, owner_map, mode_counts, helmholtz):
    highest = lax.Precision.HIGHEST
    components, reals_dev, band_modes, rows_ht, columns = velocity.shape
    kz_modes = columns // 2
    forward, backward = spanwise_tables(kz_modes, 4 * kz_modes)
    kx_count = lax.axis_size("kx")
    ht_count = lax.axis_size("ht")
    kx_total = band_modes * kx_count
    realizations = reals_dev * lax.axis_size("real")
    owners = kx_count * ht_count
    slots_dev = kz_modes // owners
    width_out = slots_dev * 2 * rows_ht
    low_members = low_index.shape[0]
    band_start = lax.axis_index("kx") * band_modes
    global_modes = band_start + jnp.arange(band_modes, dtype=jnp.int32)
    low_select = (low_index[:, None] == global_modes[None, :]).astype(jnp.float32)
    high_mask = 1.0 - jnp.sum(low_select, axis=0)
    offsets = (neighbours - global_modes[:, None] + kx_total // 2) % kx_total - kx_total // 2
    local_partner = jnp.arange(band_modes, dtype=jnp.int32)[:, None] + band_modes + offsets
    column_mask = ((jnp.arange(columns) // 2)[None, :] < mode_counts[:, None]).astype(jnp.float32)
    inverse_map = (
        jnp.zeros((kz_modes,), jnp.int32).at[owner_map].set(jnp.arange(kz_modes, dtype=jnp.int32))
    )
    current = velocity
    physical = jnp.dot(current, forward, precision=highest)
    extended = extended_2(physical, (("kx", 2),), band_modes)
    own_low = jnp.einsum("jm,crmyz->crjyz", low_select, physical, precision=highest)
    low_fields = lax.psum(own_low, "kx")
    high_low = jnp.zeros_like(physical)
    stresses = []
    for member in range(low_members):
        partner = jnp.take(extended, local_partner[:, member], axis=2)
        low_one = low_fields[:, :, member : member + 1]
        high_low = high_low + low_one * partner[1:2] + partner * low_one[1:2]
        weighted = physical * (partner[1:2] * high_mask[None, None, :, None, None])
        stresses.append(jnp.sum(weighted, axis=(1, 2)))
    stress = jnp.stack(stresses, axis=1)
    nonlinear = jnp.dot(high_low, backward, precision=highest)
    summed = lax.psum(stress, ("kx", "real"))
    low_forcing = jnp.dot(summed / realizations, backward, precision=highest)
    forcing = nonlinear * high_mask[None, None, :, None, None]
    forcing = (
        forcing + jnp.einsum("jm,cjyk->cmyk", low_select, low_forcing, precision=highest)[:, None]
    )
    forcing = forcing * column_mask[None, None, :, None, :]
    updated = current + dt_step * forcing
    slotted = jnp.take(
        updated.reshape(components, reals_dev, band_modes, rows_ht, kz_modes, 2), owner_map, axis=4
    )
    outgoing = slotted.reshape(components, reals_dev, band_modes, rows_ht, owners, slots_dev, 2)
    outgoing = outgoing.transpose(0, 1, 2, 4, 5, 6, 3)
    flat_out = outgoing.reshape(components, reals_dev, band_modes, owners, width_out)
    applied = apply_inverse(
        lax.all_to_all(flat_out, ("kx", "ht"), split_axis=3, concat_axis=3, tiled=True),
        helmholtz,
        kx_count,
        ht_count,
        slots_dev,
        rows_ht,
    )
    returned = lax.all_to_all(applied, ("kx", "ht"), split_axis=3, concat_axis=3, tiled=True)
    restored = returned.reshape(components, reals_dev, band_modes, owners, slots_dev, 2, rows_ht)
    restored = restored.transpose(0, 1, 2, 6, 3, 4, 5).reshape(
        components, reals_dev, band_modes, rows_ht, kz_modes, 2
    )
    current = jnp.take(restored, inverse_map, axis=4).reshape(
        components, reals_dev, band_modes, rows_ht, columns
    )
    return current


def solution(mesh):
    in_specs = (
        P(None, "real", "kx", "ht", None),
        P(),
        P("kx", None),
        P(),
        P("kx"),
        P(("kx", "ht"), None, None),
    )
    out_specs = P(None, "real", "kx", "ht", None)
    return jax.shard_map(local, mesh=mesh, in_specs=in_specs, out_specs=out_specs, check_vma=False)
```

profile of v0, /device:TPU:1, one launch (start us, length us, event | category | flops | bytes accessed | tf_op | source)
XLA Modules:
  0.0 327.1 jit_solution(15920989410416831472)
XLA Ops:
  6.6 2.4 fusion.12
  9.0 2.5 collective-permute-start
  11.5 4.0 %collective-permute-start.1 = (f32[3,1,4,64,256]{4,3,2,0,1:T(8,128)S(1)}, f32[3,1,4,64,256]{4,3,2,0,1:T(8,128)}, u32[]{:S(2)}, u32[]{:S(2)}) collective-permute-start(f32[3,1,4,64,256]{4,3,2,0,1:T(8,128)S(1)} %bitcast.259), channel_id=1, source_target_pairs={{32,0},{64,32},{96,64},{128,96},{160,128},{192,160},{224,192},{0,2... | collective-permute-start | bytes 2359304 | tf_op jit(solution)/shard_map/ppermute | solution.py:18
  15.6 3.1 convolution_bitcast_fusion
  19.8 12.9 %collective-permute-done = f32[3,1,4,64,256]{4,3,2,0,1:T(8,128)S(1)} collective-permute-done((f32[3,1,4,64,256]{4,3,2,0,1:T(8,128)S(1)}, f32[3,1,4,64,256]{4,3,2,0,1:T(8,128)S(1)}, u32[]{:S(2)}, u32[]{:S(2)}) %collective-permute-start) | collective-permute-done | bytes 786464 | tf_op jit(solution)/shard_map/ppermute | solution.py:15
  32.7 0.9 copy-done.16
  33.6 1.8 maximum_bitcast_fusion
  35.4 1.6 gather_fusion.7
  37.0 1.5 gather_fusion.5
  38.5 1.5 gather_fusion.4
  40.0 1.5 gather_fusion.3
  41.5 1.5 gather_fusion.2
  43.0 1.5 gather_fusion.1
  44.5 1.5 gather_fusion
  46.0 1.5 gather_fusion.6
  47.5 1.4 bitcast_select_fusion.2
  48.9 1.3 bitcast_select_fusion.4
  50.8 0.6 copy-done.10
  52.1 1.4 multiply_bitcast_fusion.1
  55.4 3.9 %stack.35 = f32[3,8,64,256]{3,1,2,0:T(8,128)} concatenate(f32[3,1,64,256]{3,1,2,0:T(1,128)S(1)} %stack.27, f32[3,1,64,256]{3,1,2,0:T(1,128)S(1)} %stack.28, f32[3,1,64,256]{3,1,2,0:T(1,128)S(1)} %stack.29, f32[3,1,64,256]{3,1,2,0:T(1,128)S(1)} %stack.30, f32[3,1,64,256]{3,1,2,0:T(1,128)S(1)} %stack.31, f32[3,1,64,256]{3,1,2,0:T(1,128)S(1)} %stack.32, ...), dimensions={1} | concatenate | bytes 3145728 | tf_op jit(solution)/shard_map/stack | solution.py:89
  60.4 35.1 %all-reduce.3.cloned.1.call-done = f32[3,1,8,64,256]{4,2,3,0,1:T(8,128)} async-done(((f32[3,1,8,64,256]{4,2,3,0,1:T(8,128)}), f32[3,1,8,64,256]{4,2,3,0,1:T(8,128)}) %all-reduce.3.cloned.1.call-update) | async-done | bytes 1572880 | tf_op jit(solution)/shard_map/psum | solution.py:80
  95.5 7.7 %fusion.51 = (f32[3,1,1,64,256]{4,2,3,0,1:T(1,128)S(1)}, f32[3,1,1,64,256]{4,2,3,0,1:T(1,128)S(1)}, f32[3,1,1,64,256]{4,2,3,0,1:T(1,128)S(1)}, f32[3,1,1,64,256]...) fusion(f32[3,1,8,64,256]{4,2,3,0,1:T(8,128)} %all-reduce.3.clon, ...), kind=kLoop, calls=%fused_computation.172 | loop fusion | bytes 3145728 | tf_op jit(solution)/shard_map/slice | solution.py:85
  103.2 0.7 copy.102
  103.8 0.7 copy.103
  104.5 0.7 copy.104
  105.2 0.7 copy.105
  105.9 0.7 copy.106
  106.6 0.7 copy.107
  107.3 0.7 copy.108
  108.0 0.7 copy.109
  108.7 3.5 %fusion.52 = (f32[1,1,1,64,256]{4,2,3,0,1:T(1,128)S(1)}, f32[1,1,1,64,256]{4,2,3,0,1:T(1,128)S(1)}, f32[1,1,1,64,256]{4,2,3,0,1:T(1,128)S(1)}, f32[1,1,1,64,256]...) fusion(f32[3,1,8,64,256]{4,2,3,0,1:T(8,128)} %all-reduce.3.clon, ...), kind=kLoop, calls=%fused_computation.173 | loop fusion | bytes 1048576 | tf_op jit(solution)/shard_map/slice | solution.py:86
  112.2 0.6 copy.112
  113.5 0.6 copy.114
  115.3 0.6 copy.117
  116.0 133.7 %all-reduce.5.cloned.1.call-done = f32[3,8,64,256]{3,1,2,0:T(8,128)} async-done(((f32[3,8,64,256]{3,1,2,0:T(8,128)}), f32[3,8,64,256]{3,1,2,0:T(8,128)}) %all-reduce.5.cloned.1.call-update) | async-done | bytes 1572880 | tf_op jit(solution)/shard_map/psum | solution.py:91
  249.7 3.5 %fusion = f32[3,8,64,128]{3,1,2,0:T(8,128)S(1)} fusion(f32[3,8,64,256]{3,1,2,0:T(8,128)} %all-reduce.5.cloned.1.call-done, f32[256]{0:T(256)S(1)} %convert_multiply_fusion, f32[128]{0:T(128)} %copy-done.17, pred[128]{0:T(512)(128)(4,1)S(1)} %fusion.42), kind=kOutput, calls=%fused_computation.12 | convolution fusion | flops 604504064 | bytes 2360960 | tf_op jit(solution)/shard_map/dot_general | solution.py:92
  253.2 1.2 fusion.50
  254.4 5.9 %fusion.6 = f32[3,1,4,64,128]{4,3,2,0,1:T(8,128)} fusion(f32[3,1,4,64,128]{4,3,2,1,0:T(8,128)S(1)} %copy-done.14, f32[3,64,128,4]{2,3,1,0:T(4,128)S(1)} %fusion.50, f32[4,128]{1,0:T(4,128)S(1)} %compare_convert_fusion.1, f32[4]{0:T(128)} %copy-done.27, f32[256]{0:T(256)S(1)} %convert_multiply_fusion, f32[128]{0:T(128)} %copy-done.17, ...), kind=kOutput, calls=%fused_computation.21 | convolution fusion | flops 310280192 | bytes 11669168 | tf_op jit(solution)/shard_map/dot_general | solution.py:90
  260.3 1.3 copy.38
  262.1 1.0 gather_fusion.8
  264.4 27.5 %all_to_all.10 = f32[3,1,4,64,128]{4,2,0,1,3:T(4,128)S(1)} all-to-all(f32[3,1,4,64,128]{4,2,0,1,3:T(4,128)S(1)} %reshape.457), channel_id=1, replica_groups=mesh['kx'=8,'ht'=8,'real'=4] {'kx','ht'}, dimensions={3} | all-to-all | bytes 786432 | tf_op jit(solution)/shard_map/all_to_all | solution.py:106
  292.8 1.5 convolution_bitcast_fusion.1
  294.9 1.3 reshape.459
  296.2 5.5 %all-to-all-start.1 = ((f32[3,1,4,64,128]{4,2,0,1,3:T(4,128)}), f32[3,1,4,64,128]{4,2,0,1,3:T(4,128)S(1)}, u32[]{:S(2)}, u32[]{:S(2)}) async-start(f32[3,1,4,64,128]{4,2,0,1,3:T(4,128)} %reshape.459), calls=%async_computation.1 | async-start | bytes 786432 | tf_op jit(solution)/shard_map/all_to_all | solution.py:113
  301.6 0.9 scatter_custom_fusion
  302.6 14.2 %all-to-all-done.1 = f32[3,1,4,64,128]{4,2,0,1,3:T(4,128)S(1)} async-done(((f32[3,1,4,64,128]{4,2,0,1,3:T(4,128)}), f32[3,1,4,64,128]{4,2,0,1,3:T(4,128)S(1)}, u32[]{:S(2)}, u32[]{:S(2)}) %all-to-all-start.1) | async-done | bytes 393248 | tf_op jit(solution)/shard_map/all_to_all | solution.py:113
  317.5 1.1 gather_fusion.9
  319.3 1.0 copy.49
  (145 shorter events, 11.2 us)
Async XLA Ops:
  6.5 286.2 %copy-start = (f32[1,512,512]{2,1,0:T(8,128)S(1)}, f32[1,512,512]{2,1,0:T(8,128)}, u32[]{:S(2)}) copy-start(f32[1,512,512]{2,1,0:T(8,128)} %param.15) | copy-start | bytes 3145732
  6.5 89.0 %all-reduce.3.cloned.1.call-start = ((), (), s32[]{:S(2)}) async-start(), calls=%async_computation.2 | async-start | bytes 3145728 | tf_op jit(solution)/shard_map/psum | solution.py:80
  6.6 12.2 %copy-start.17 = (f32[128]{0:T(128)}, f32[128]{0:T(128)S(1)}, u32[]{:S(2)}) copy-start(f32[128]{0:T(128)S(1)} %fusion.45) | copy-start | bytes 1540
  6.6 12.2 %copy-start.28 = (s32[4,8]{1,0:T(4,128)S(1)}, s32[4,8]{1,0:T(4,128)}, u32[]{:S(2)}) copy-start(s32[4,8]{1,0:T(4,128)} %param.12) | copy-start | bytes 388
  6.6 13.0 %copy-start.29 = (s32[8]{0:T(128)S(1)}, s32[8]{0:T(128)}, u32[]{:S(2)}) copy-start(s32[8]{0:T(128)} %param.11) | copy-start | bytes 100
  9.0 23.7 %copy-start.1 = (f32[256,3,4,64]{0,3,2,1:T(8,128)}, f32[256,3,4,64]{0,3,2,1:T(8,128)S(1)}, u32[]{:S(2)}) copy-start(f32[256,3,4,64]{0,3,2,1:T(8,128)S(1)} %fusion.12) | copy-start | bytes 2359300
  9.0 23.7 %collective-permute-start = (f32[3,1,4,64,256]{4,3,2,0,1:T(8,128)S(1)}, f32[3,1,4,64,256]{4,3,2,0,1:T(8,128)S(1)}, u32[]{:S(2)}, u32[]{:S(2)}) collective-permute-start(f32[3,1,4,64,256]{4,3,2,0,1:T(8,128)S(1)} %bitcast.258), channel_id=1, source_target_pairs={{0,32},{32,64},{64,96},{96,128},{128,160},{160,192},{192,224},{224... | collective-permute-start | bytes 2359304 | tf_op jit(solution)/shard_map/ppermute | solution.py:15
  11.5 22.1 %collective-permute-start.1 = (f32[3,1,4,64,256]{4,3,2,0,1:T(8,128)S(1)}, f32[3,1,4,64,256]{4,3,2,0,1:T(8,128)}, u32[]{:S(2)}, u32[]{:S(2)}) collective-permute-start(f32[3,1,4,64,256]{4,3,2,0,1:T(8,128)S(1)} %bitcast.259), channel_id=1, source_target_pairs={{32,0},{64,32},{96,64},{128,96},{160,128},{192,160},{224,192},{0,2... | collective-permute-start | bytes 2359304 | tf_op jit(solution)/shard_map/ppermute | solution.py:18
  15.6 19.9 %copy-start.18 = (s32[4]{0:T(128)}, s32[4]{0:T(128)S(1)}, u32[]{:S(2)}) copy-start(s32[4]{0:T(128)S(1)} %get-tuple-element.70) | copy-start | bytes 52
  18.8 230.9 %all-reduce.5.cloned.1.call-start = ((), (), s32[]{:S(2)}) async-start(), calls=%async_computation.3 | async-start | bytes 3145728 | tf_op jit(solution)/shard_map/psum | solution.py:91
  19.2 28.2 %copy-start.19 = (pred[4]{0:T(512)(128)(4,1)}, pred[4]{0:T(512)(128)(4,1)S(1)}, u32[]{:S(2)}) copy-start(pred[4]{0:T(512)(128)(4,1)S(1)} %compare_and_fusion.2) | copy-start | bytes 16
  19.3 29.6 %copy-start.20 = (pred[4]{0:T(512)(128)(4,1)}, pred[4]{0:T(512)(128)(4,1)S(1)}, u32[]{:S(2)}) copy-start(pred[4]{0:T(512)(128)(4,1)S(1)} %compare_and_fusion.4) | copy-start | bytes 16
  19.3 30.9 %copy-start.21 = (pred[4]{0:T(512)(128)(4,1)}, pred[4]{0:T(512)(128)(4,1)S(1)}, u32[]{:S(2)}) copy-start(pred[4]{0:T(512)(128)(4,1)S(1)} %compare_and_fusion.5) | copy-start | bytes 16
  19.3 31.1 %copy-start.22 = (pred[4]{0:T(512)(128)(4,1)}, pred[4]{0:T(512)(128)(4,1)S(1)}, u32[]{:S(2)}) copy-start(pred[4]{0:T(512)(128)(4,1)S(1)} %compare_and_fusion.6) | copy-start | bytes 16
  19.4 31.2 %copy-start.23 = (pred[4]{0:T(512)(128)(4,1)}, pred[4]{0:T(512)(128)(4,1)S(1)}, u32[]{:S(2)}) copy-start(pred[4]{0:T(512)(128)(4,1)S(1)} %compare_and_fusion.7) | copy-start | bytes 16
  19.4 31.4 %copy-start.24 = (pred[4]{0:T(512)(128)(4,1)}, pred[4]{0:T(512)(128)(4,1)S(1)}, u32[]{:S(2)}) copy-start(pred[4]{0:T(512)(128)(4,1)S(1)} %compare_and_fusion.8) | copy-start | bytes 16
  19.7 31.8 %copy-start.25 = (pred[4]{0:T(512)(128)(4,1)}, pred[4]{0:T(512)(128)(4,1)S(1)}, u32[]{:S(2)}) copy-start(pred[4]{0:T(512)(128)(4,1)S(1)} %compare_and_fusion.9) | copy-start | bytes 16
  19.8 32.1 %copy-start.26 = (pred[4]{0:T(512)(128)(4,1)}, pred[4]{0:T(512)(128)(4,1)S(1)}, u32[]{:S(2)}) copy-start(pred[4]{0:T(512)(128)(4,1)S(1)} %compare_and_fusion.3) | copy-start | bytes 16
  19.8 32.3 %copy-start.27 = (f32[4]{0:T(128)}, f32[4]{0:T(128)S(1)}, u32[]{:S(2)}) copy-start(f32[4]{0:T(128)S(1)} %broadcast_subtract_fusion) | copy-start | bytes 52
  32.7 0.9 copy-start.16
  47.5 2.8 copy-start.5
  47.5 3.0 copy-start.6
  48.9 1.7 copy-start.8
  50.3 1.2 copy-start.10
  50.4 1.2 copy-start.12
  50.6 1.4 copy-start.13
  52.1 1.6 copy-start.2
  55.3 3.9 %copy-start.33 = (s32[64]{0:T(128)S(1)}, s32[64]{0:T(128)}, u32[]{:S(2)}) copy-start(s32[64]{0:T(128)} %param.13) | copy-start | bytes 772
  55.4 5.0 %copy-start.32 = (s32[4]{0:T(128)S(1)}, s32[4]{0:T(128)}, u32[]{:S(2)}) copy-start(s32[4]{0:T(128)} %param.14) | copy-start | bytes 52
  59.3 0.5 copy-start.31
  112.2 142.2 %copy-start.3 = (f32[4,3,64,256]{3,2,1,0:T(8,128)S(1)}, f32[4,3,64,256]{3,2,1,0:T(8,128)}, u32[]{:S(2)}) copy-start(f32[4,3,64,256]{3,2,1,0:T(8,128)} %gather_fusion.7) | copy-start | bytes 2359300
  112.2 142.2 %copy-start.4 = (f32[4,3,64,256]{3,2,1,0:T(8,128)S(1)}, f32[4,3,64,256]{3,2,1,0:T(8,128)}, u32[]{:S(2)}) copy-start(f32[4,3,64,256]{3,2,1,0:T(8,128)} %gather_fusion.5) | copy-start | bytes 2359300
  249.7 4.7 %copy-start.7 = (f32[4,3,64,256]{3,2,1,0:T(8,128)S(1)}, f32[4,3,64,256]{3,2,1,0:T(8,128)}, u32[]{:S(2)}) copy-start(f32[4,3,64,256]{3,2,1,0:T(8,128)} %gather_fusion.3) | copy-start | bytes 2359300
  249.7 4.7 %copy-start.9 = (f32[4,3,64,256]{3,2,1,0:T(8,128)S(1)}, f32[4,3,64,256]{3,2,1,0:T(8,128)}, u32[]{:S(2)}) copy-start(f32[4,3,64,256]{3,2,1,0:T(8,128)} %gather_fusion.2) | copy-start | bytes 2359300
  249.7 4.7 %copy-start.11 = (f32[4,3,64,256]{3,2,1,0:T(8,128)S(1)}, f32[4,3,64,256]{3,2,1,0:T(8,128)}, u32[]{:S(2)}) copy-start(f32[4,3,64,256]{3,2,1,0:T(8,128)} %gather_fusion.1) | copy-start | bytes 2359300
  249.7 4.7 %copy-start.14 = (f32[3,1,4,64,128]{4,3,2,1,0:T(8,128)S(1)}, f32[3,1,4,64,128]{4,3,2,1,0:T(8,128)}, u32[]{:S(2)}) copy-start(f32[3,1,4,64,128]{4,3,2,1,0:T(8,128)} %param.10) | copy-start | bytes 1179652
  249.7 4.7 %copy-start.15 = (f32[4,64,256]{2,1,0:T(8,128)S(1)}, f32[4,64,256]{2,1,0:T(8,128)}, u32[]{:S(2)}) copy-start(f32[4,64,256]{2,1,0:T(8,128)} %get-tuple-element.40) | copy-start | bytes 786436
  262.1 1.1 copy-start.30
  296.2 20.6 %all-to-all-start.1 = ((f32[3,1,4,64,128]{4,2,0,1,3:T(4,128)}), f32[3,1,4,64,128]{4,2,0,1,3:T(4,128)S(1)}, u32[]{:S(2)}, u32[]{:S(2)}) async-start(f32[3,1,4,64,128]{4,2,0,1,3:T(4,128)} %reshape.459), calls=%async_computation.1 | async-start | bytes 786432 | tf_op jit(solution)/shard_map/all_to_all | solution.py:113
Sparse Core Ops, SparseCore 0:
  18.9 76.5 all-reduce.2
  98.9 150.7 all-reduce.4
where the time goes:
time: 328 us; the launch traced here: 327 us
  waiting for transfers between devices  196 us (60%)
  local copies, waits for them, and re-layouts  50.8 us (15%)
  blocking collectives  27.5 us (8%)
  matrix products  17.6 us (5%)
  between operations  14.4 us (4%)
  starting transfers between devices  12.1 us (4%)
  other arithmetic  8.77 us (3%)
    psum x1, waiting for transfers between devices, local(): summed = lax.psum(stress, ('kx', 'real'))  134 us
    psum x1, waiting for transfers between devices, local(): low_fields = lax.psum(own_low, 'kx')  35.1 us
    all_to_all x1, blocking collectives, local(): lax.all_to_all(flat_out, ('kx', 'ht'), split_axis=3, concat_axis=3, tiled...  27.5 us
    all_to_all x1, waiting for transfers between devices, local(): lax.all_to_all(applied, ('kx', 'ht'), split_axis=3, concat_axis=3, tiled=...  14.2 us
    ppermute x1, waiting for transfers between devices, extended_2(): lax.ppermute(lax.slice_in_dim(block, block.shape[dim] - width, None, axis...  12.9 us
    gather x8, local copies, waits for them, and re-layouts, local(): partner = jnp.take(extended, local_partner[:, member], axis=2)  12 us
    unnamed x84, local copies, waits for them, and re-layouts  11.8 us
    slice x1, local copies, waits for them, and re-layouts, local(): low_one = low_fields[:, :, member:member + 1]  7.67 us
  transfers between devices with their start and end apart: 5, of which 4 were waited for; matrix products, arithmetic and copies ran while one was open for 15% of the time, Pallas kernels for 0%

commit v1 on v0

--- a/solution.py
+++ b/solution.py
@@ -1,9 +1,34 @@
+import functools
 import jax
 import jax.numpy as jnp
 from jax import lax
 from jax.sharding import PartitionSpec as P
 
 dt_step = 0.1
+
+
+def _lead_members_all(field, group_axis):
+    size_here = lax.axis_size(group_axis)
+
+    def guide_counts_over_axis(all_rows, arr_out):
+        if arr_out >= size_here:
+            return all_rows
+        r2 = guide_counts_over_axis(
+            all_rows
+            + lax.ppermute(
+                all_rows,
+                group_axis,
+                perm=tuple(((src_i, src_i ^ arr_out) for src_i in range(size_here))),
+            ),
+            2 * arr_out,
+        )
+        return r2
+
+    outcome_arr = guide_counts_over_axis(field, 1)
+    return outcome_arr
+
+
+recover_the_loads = functools.partial(_lead_members_all, group_axis="kx")
 
 
 def extended_2(block, sides, width):
@@ -77,7 +102,7 @@
     physical = jnp.dot(current, forward, precision=highest)
     extended = extended_2(physical, (("kx", 2),), band_modes)
     own_low = jnp.einsum("jm,crmyz->crjyz", low_select, physical, precision=highest)
-    low_fields = lax.psum(own_low, "kx")
+    low_fields = recover_the_loads(own_low)
     high_low = jnp.zeros_like(physical)
     stresses = []
     for member in range(low_members):

time: 328 us -> 378 us (1.15)
  waiting for transfers between devices: 196 us -> 246 us
  local copies, waits for them, and re-layouts: 50.8 us -> 31.3 us
  other arithmetic: 8.77 us -> 23.9 us
  starting transfers between devices: 12.1 us -> 21.3 us
  matrix products: 17.6 us -> 13.3 us
    ppermute x0 -> x3, waiting for transfers between devices: none -> 75 us  [guide_counts_over_axis(): lax.ppermute(all_rows, group_axis, perm=tuple(((src_i, src_i ^ arr_out) f...]
    psum x1 -> x0, waiting for transfers between devices: 35.1 us -> none  [local(): low_fields = lax.psum(own_low, 'kx')]
    psum x1, waiting for transfers between devices: 134 us -> 143 us  [local(): summed = lax.psum(stress, ('kx', 'real'))]
    ppermute x0 -> x3, starting transfers between devices: none -> 9.31 us  [guide_counts_over_axis(): lax.ppermute(all_rows, group_axis, perm=tuple(((src_i, src_i ^ arr_out) f...]
    unnamed x84 -> x70, local copies, waits for them, and re-layouts: 11.8 us -> 2.91 us
    select_n x16, other arithmetic: 3.58 us -> 11 us  [local(): partner = jnp.take(extended, local_partner[:, member], axis=2)]
    add x0 -> x3, other arithmetic: none -> 6.92 us  [guide_counts_over_axis(): all_rows + lax.ppermute(all_rows, group_axis, perm=tuple(((src_i, src_i ^...]
    slice x1, local copies, waits for them, and re-layouts: 7.67 us -> 1.45 us  [local(): low_one = low_fields[:, :, member:member + 1]]
  transfers between devices with their start and end apart: 5 -> 7, of which waited for: 4 -> 5; matrix products, arithmetic and copies ran while one was open for 15% -> 12% of each run, Pallas kernels for 0% -> 0%
where the time goes in v1:
time: 378 us; the launch traced here: 377 us
  waiting for transfers between devices  246 us (65%)
  local copies, waits for them, and re-layouts  31.3 us (8%)
  blocking collectives  27.5 us (7%)
  other arithmetic  23.9 us (6%)
  starting transfers between devices  21.3 us (6%)
  between operations  14.3 us (4%)
  matrix products  13.3 us (4%)
    psum x1, waiting for transfers between devices, local(): summed = lax.psum(stress, ('kx', 'real'))  143 us
    ppermute x3, waiting for transfers between devices, guide_counts_over_axis(): lax.ppermute(all_rows, group_axis, perm=tuple(((src_i, src_i ^ arr_out) f...  75 us
    all_to_all x1, blocking collectives, local(): lax.all_to_all(flat_out, ('kx', 'ht'), split_axis=3, concat_axis=3, tiled...  27.5 us
    all_to_all x1, waiting for transfers between devices, local(): lax.all_to_all(applied, ('kx', 'ht'), split_axis=3, concat_axis=3, tiled=...  14.3 us
    ppermute x1, waiting for transfers between devices, extended_2(): lax.ppermute(lax.slice_in_dim(block, block.shape[dim] - width, None, axis...  13.1 us
    gather x8, local copies, waits for them, and re-layouts, local(): partner = jnp.take(extended, local_partner[:, member], axis=2)  12 us
    select_n x16, other arithmetic, local(): partner = jnp.take(extended, local_partner[:, member], axis=2)  11 us
    ppermute x3, starting transfers between devices, guide_counts_over_axis(): lax.ppermute(all_rows, group_axis, perm=tuple(((src_i, src_i ^ arr_out) f...  9.31 us
  transfers between devices with their start and end apart: 7, of which 5 were waited for; matrix products, arithmetic and copies ran while one was open for 12% of the time, Pallas kernels for 0%

profile of v1, /device:TPU:1, one launch (start us, length us, event | category | flops | bytes accessed | tf_op | source)
XLA Modules:
  0.0 377.1 jit_solution(3601382060062478295)
XLA Ops:
  6.6 2.4 fusion.12
  9.0 2.5 collective-permute-start.3
  11.5 4.0 %collective-permute-start.4 = (f32[3,1,4,64,256]{4,3,2,0,1:T(8,128)S(1)}, f32[3,1,4,64,256]{4,3,2,0,1:T(8,128)}, u32[]{:S(2)}, u32[]{:S(2)}) collective-permute-start(f32[3,1,4,64,256]{4,3,2,0,1:T(8,128)S(1)} %bitcast.259), channel_id=1, source_target_pairs={{32,0},{64,32},{96,64},{128,96},{160,128},{192,160},{224,192},{0,2... | collective-permute-start | bytes 2359304 | tf_op jit(solution)/shard_map/ppermute | solution.py:43
  15.6 3.1 convolution_bitcast_fusion
  19.6 13.1 %collective-permute-done.3 = f32[3,1,4,64,256]{4,3,2,0,1:T(8,128)S(1)} collective-permute-done((f32[3,1,4,64,256]{4,3,2,0,1:T(8,128)S(1)}, f32[3,1,4,64,256]{4,3,2,0,1:T(8,128)S(1)}, u32[]{:S(2)}, u32[]{:S(2)}) %collective-permute-start.3) | collective-permute-done | bytes 786464 | tf_op jit(solution)/shard_map/ppermute | solution.py:40
  32.7 0.9 copy-done.22
  33.6 1.8 maximum_bitcast_fusion
  35.4 1.5 gather_fusion.7
  36.9 1.6 gather_fusion.5
  38.5 1.5 gather_fusion.4
  40.0 1.5 gather_fusion.3
  41.5 1.5 gather_fusion.2
  42.9 1.5 gather_fusion.1
  44.5 1.5 gather_fusion
  46.0 2.3 bitcast_select_fusion.2
  48.2 2.2 bitcast_select_fusion.4
  50.5 1.1 bitcast_select_fusion.5
  51.5 1.1 bitcast_select_fusion.6
  52.6 1.0 bitcast_select_fusion.7
  53.6 1.0 bitcast_select_fusion.8
  54.7 9.2 %collective-permute-done = f32[3,1,8,64,256]{4,2,3,0,1:T(8,128)} collective-permute-done((f32[3,1,8,64,256]{4,2,3,0,1:T(8,128)}, f32[3,1,8,64,256]{4,2,3,0,1:T(8,128)}, u32[]{:S(2)}, u32[]{:S(2)}) %collective-permute-start) | collective-permute-done | bytes 1572896 | tf_op jit(solution)/shard_map/ppermute | solution.py:18
  63.8 3.2 add.144
  67.1 4.3 %collective-permute-start.1 = (f32[3,1,8,64,256]{4,2,3,0,1:T(8,128)}, f32[3,1,8,64,256]{4,2,3,0,1:T(8,128)}, u32[]{:S(2)}, u32[]{:S(2)}) collective-permute-start(f32[3,1,8,64,256]{4,2,3,0,1:T(8,128)} %add.144), channel_id=1, source_target_pairs={{0,64},{32,96},{64,0},{96,32},{128,192},{160,224},{192,128},{224,1... | collective-permute-start | bytes 4718600 | tf_op jit(solution)/shard_map/ppermute | solution.py:18
  71.4 1.0 bitcast_select_fusion.9
  72.4 1.5 gather_fusion.6
  73.9 1.3 bitcast_select_fusion.3
  75.2 2.7 multiply_bitcast_fusion.1
  79.5 3.7 stack.35
  83.3 65.8 %collective-permute-done.1 = f32[3,1,8,64,256]{4,2,3,0,1:T(8,128)} collective-permute-done((f32[3,1,8,64,256]{4,2,3,0,1:T(8,128)}, f32[3,1,8,64,256]{4,2,3,0,1:T(8,128)}, u32[]{:S(2)}, u32[]{:S(2)}) %collective-permute-start.1) | collective-permute-done | bytes 1572896 | tf_op jit(solution)/shard_map/ppermute | solution.py:18
  149.1 2.1 add.145
  151.1 5.0 %collective-permute-start.2 = (f32[3,1,8,64,256]{4,2,3,0,1:T(8,128)S(1)}, f32[3,1,8,64,256]{4,2,3,0,1:T(8,128)}, u32[]{:S(2)}, u32[]{:S(2)}) collective-permute-start(f32[3,1,8,64,256]{4,2,3,0,1:T(8,128)S(1)} %add.145), channel_id=1, source_target_pairs={{0,128},{32,160},{64,192},{96,224},{128,0},{160,32},{192,64},{224,... | collective-permute-start | bytes 4718600 | tf_op jit(solution)/shard_map/ppermute | solution.py:18
  156.3 143.1 %all-reduce.2.cloned.1.call-done = f32[3,8,64,256]{3,1,2,0:T(8,128)} async-done(((f32[3,8,64,256]{3,1,2,0:T(8,128)}), f32[3,8,64,256]{3,1,2,0:T(8,128)}) %all-reduce.2.cloned.1.call-update) | async-done | bytes 1572880 | tf_op jit(solution)/shard_map/psum | solution.py:116
  299.3 3.3 fusion
  302.7 0.5 fusion.50
  303.2 1.6 add.146
  304.9 1.5 fusion.51
  308.9 2.4 fusion.6
  312.2 1.0 gather_fusion.8
  313.9 0.6 reshape.457
  314.4 27.5 %all_to_all.10 = f32[3,1,4,64,128]{4,2,0,1,3:T(4,128)S(1)} all-to-all(f32[3,1,4,64,128]{4,2,0,1,3:T(4,128)S(1)} %reshape.457), channel_id=1, replica_groups=mesh['kx'=8,'ht'=8,'real'=4] {'kx','ht'}, dimensions={3} | all-to-all | bytes 786432 | tf_op jit(solution)/shard_map/all_to_all | solution.py:131
  342.8 1.5 convolution_bitcast_fusion.1
  344.3 0.6 copy.56
  344.9 1.3 reshape.459
  346.2 5.4 %all-to-all-start.1 = ((f32[3,1,4,64,128]{4,2,0,1,3:T(4,128)}), f32[3,1,4,64,128]{4,2,0,1,3:T(4,128)S(1)}, u32[]{:S(2)}, u32[]{:S(2)}) async-start(f32[3,1,4,64,128]{4,2,0,1,3:T(4,128)} %reshape.459), calls=%async_computation.1 | async-start | bytes 786432 | tf_op jit(solution)/shard_map/all_to_all | solution.py:138
  351.7 0.8 scatter_custom_fusion
  352.5 14.3 %all-to-all-done.1 = f32[3,1,4,64,128]{4,2,0,1,3:T(4,128)S(1)} async-done(((f32[3,1,4,64,128]{4,2,0,1,3:T(4,128)}), f32[3,1,4,64,128]{4,2,0,1,3:T(4,128)S(1)}, u32[]{:S(2)}, u32[]{:S(2)}) %all-to-all-start.1) | async-done | bytes 393248 | tf_op jit(solution)/shard_map/all_to_all | solution.py:138
  367.6 1.1 gather_fusion.9
  369.3 1.0 copy.49
  (137 shorter events, 8.4 us)
Async XLA Ops:
  6.5 336.3 %copy-start = (f32[1,512,512]{2,1,0:T(8,128)S(1)}, f32[1,512,512]{2,1,0:T(8,128)}, u32[]{:S(2)}) copy-start(f32[1,512,512]{2,1,0:T(8,128)} %param.15) | copy-start | bytes 3145732
  6.5 12.8 %copy-start.24 = (s32[8]{0:T(128)S(1)}, s32[8]{0:T(128)}, u32[]{:S(2)}) copy-start(s32[8]{0:T(128)} %param.11) | copy-start | bytes 100
  6.5 12.2 %copy-start.23 = (s32[4,8]{1,0:T(4,128)S(1)}, s32[4,8]{1,0:T(4,128)}, u32[]{:S(2)}) copy-start(s32[4,8]{1,0:T(4,128)} %param.12) | copy-start | bytes 388
  6.5 292.8 %all-reduce.2.cloned.1.call-start = ((), (), s32[]{:S(2)}) async-start(), calls=%async_computation.2 | async-start | bytes 3145728 | tf_op jit(solution)/shard_map/psum | solution.py:116
  9.0 23.7 %copy-start.1 = (f32[256,3,4,64]{0,3,2,1:T(8,128)}, f32[256,3,4,64]{0,3,2,1:T(8,128)S(1)}, u32[]{:S(2)}) copy-start(f32[256,3,4,64]{0,3,2,1:T(8,128)S(1)} %fusion.12) | copy-start | bytes 2359300
  9.0 23.7 %collective-permute-start.3 = (f32[3,1,4,64,256]{4,3,2,0,1:T(8,128)S(1)}, f32[3,1,4,64,256]{4,3,2,0,1:T(8,128)S(1)}, u32[]{:S(2)}, u32[]{:S(2)}) collective-permute-start(f32[3,1,4,64,256]{4,3,2,0,1:T(8,128)S(1)} %bitcast.258), channel_id=1, source_target_pairs={{0,32},{32,64},{64,96},{96,128},{128,160},{160,192},{192,224},{224... | collective-permute-start | bytes 2359304 | tf_op jit(solution)/shard_map/ppermute | solution.py:40
  11.5 22.1 %collective-permute-start.4 = (f32[3,1,4,64,256]{4,3,2,0,1:T(8,128)S(1)}, f32[3,1,4,64,256]{4,3,2,0,1:T(8,128)}, u32[]{:S(2)}, u32[]{:S(2)}) collective-permute-start(f32[3,1,4,64,256]{4,3,2,0,1:T(8,128)S(1)} %bitcast.259), channel_id=1, source_target_pairs={{32,0},{64,32},{96,64},{128,96},{160,128},{192,160},{224,192},{0,2... | collective-permute-start | bytes 2359304 | tf_op jit(solution)/shard_map/ppermute | solution.py:43
  18.7 45.1 %collective-permute-start = (f32[3,1,8,64,256]{4,2,3,0,1:T(8,128)}, f32[3,1,8,64,256]{4,2,3,0,1:T(8,128)}, u32[]{:S(2)}, u32[]{:S(2)}) collective-permute-start(f32[3,1,8,64,256]{4,2,3,0,1:T(8,128)} %convolution_bitcast_fusion), channel_id=1, source_target_pairs={{0,32},{32,0},{64,96},{96,64},{128,160},{160,128},{192,224},{224,1... | collective-permute-start | bytes 4718600 | tf_op jit(solution)/shard_map/ppermute | solution.py:18
  32.7 0.9 copy-start.22
  46.0 4.5 %copy-start.5 = (f32[4,3,64,256]{3,2,1,0:T(8,128)S(1)}, f32[4,3,64,256]{3,2,1,0:T(8,128)}, u32[]{:S(2)}) copy-start(f32[4,3,64,256]{3,2,1,0:T(8,128)} %gather_fusion.4) | copy-start | bytes 2359300
  46.0 5.6 %copy-start.7 = (f32[4,3,64,256]{3,2,1,0:T(8,128)S(1)}, f32[4,3,64,256]{3,2,1,0:T(8,128)}, u32[]{:S(2)}) copy-start(f32[4,3,64,256]{3,2,1,0:T(8,128)} %gather_fusion.3) | copy-start | bytes 2359300
  48.2 4.4 %copy-start.9 = (f32[4,3,64,256]{3,2,1,0:T(8,128)S(1)}, f32[4,3,64,256]{3,2,1,0:T(8,128)}, u32[]{:S(2)}) copy-start(f32[4,3,64,256]{3,2,1,0:T(8,128)} %gather_fusion.2) | copy-start | bytes 2359300
  50.5 3.2 copy-start.11
  54.7 16.7 %copy-start.13 = (f32[4,3,64,256]{3,2,1,0:T(8,128)S(1)}, f32[4,3,64,256]{3,2,1,0:T(8,128)}, u32[]{:S(2)}) copy-start(f32[4,3,64,256]{3,2,1,0:T(8,128)} %gather_fusion) | copy-start | bytes 2359300
  67.1 82.0 %collective-permute-start.1 = (f32[3,1,8,64,256]{4,2,3,0,1:T(8,128)}, f32[3,1,8,64,256]{4,2,3,0,1:T(8,128)}, u32[]{:S(2)}, u32[]{:S(2)}) collective-permute-start(f32[3,1,8,64,256]{4,2,3,0,1:T(8,128)} %add.144), channel_id=1, source_target_pairs={{0,64},{32,96},{64,0},{96,32},{128,192},{160,224},{192,128},{224,1... | collective-permute-start | bytes 4718600 | tf_op jit(solution)/shard_map/ppermute | solution.py:18
  75.2 2.7 copy-start.2
  83.2 72.9 %copy-start.26 = (s32[64]{0:T(128)S(1)}, s32[64]{0:T(128)}, u32[]{:S(2)}) copy-start(s32[64]{0:T(128)} %param.13) | copy-start | bytes 772
  83.2 72.9 %copy-start.25 = (s32[4]{0:T(128)S(1)}, s32[4]{0:T(128)}, u32[]{:S(2)}) copy-start(s32[4]{0:T(128)} %param.14) | copy-start | bytes 52
  151.1 152.1 %collective-permute-start.2 = (f32[3,1,8,64,256]{4,2,3,0,1:T(8,128)S(1)}, f32[3,1,8,64,256]{4,2,3,0,1:T(8,128)}, u32[]{:S(2)}, u32[]{:S(2)}) collective-permute-start(f32[3,1,8,64,256]{4,2,3,0,1:T(8,128)S(1)} %add.145), channel_id=1, source_target_pairs={{0,128},{32,160},{64,192},{96,224},{128,0},{160,32},{192,64},{224,... | collective-permute-start | bytes 4718600 | tf_op jit(solution)/shard_map/ppermute | solution.py:18
  304.8 2.3 copy-start.14
  304.8 2.3 copy-start.15
  304.8 2.3 copy-start.17
  304.9 2.3 copy-start.18
  304.9 2.3 copy-start.19
  304.9 2.3 copy-start.20
  304.9 2.3 copy-start.21
  306.4 1.2 copy-start.12
  306.4 1.3 copy-start.16
  306.7 1.2 copy-start.3
  306.8 1.4 copy-start.4
  306.8 1.7 copy-start.6
  306.8 1.9 copy-start.8
  306.8 2.1 copy-start.10
  346.2 20.6 %all-to-all-start.1 = ((f32[3,1,4,64,128]{4,2,0,1,3:T(4,128)}), f32[3,1,4,64,128]{4,2,0,1,3:T(4,128)S(1)}, u32[]{:S(2)}, u32[]{:S(2)}) async-start(f32[3,1,4,64,128]{4,2,0,1,3:T(4,128)} %reshape.459), calls=%async_computation.1 | async-start | bytes 786432 | tf_op jit(solution)/shard_map/all_to_all | solution.py:138
Sparse Core Ops, SparseCore 0:
  83.3 215.9 all-reduce.1
